TPU v7x, 32 devices: a whole 2x2x4 slice. The times are simulated.
32 devices in a mesh: dp: 4 (over y, core), label: 8 (over z, x).
Axes of the slice: x: 2, y: 2, z: 4, core: 2. Of those that a mesh axis runs over, the one named last changes fastest.
Arguments:
- calib: bfloat16 [16384, 2688], P(('dp', 'label')), may hold values from -160 to 160
- block_weight: bfloat16 [8192, 128], P('dp', 'label'), may hold values from -0.125 to 0.125
- rest_weight: bfloat16 [8192, 2560], P('dp', 'label'), may hold values from -0.125 to 0.125
- prune_mask: int32 [8192, 128], P(('dp', 'label')), may hold values 0 or 1
Outputs:
- pruned_block: bfloat16 [8192, 128], P(('dp', 'label'))
- updated_rest: bfloat16 [8192, 2560], P('dp', 'label')
All inputs are finite; a program needn't handle non-finite values. No bound on the sum of `prune_mask` on one device may be relied on, other than what follows from the above.
Results may differ from a plain program's by a relative error of at most 0.00075.
Values may be sent and summed in bfloat16 or wider, within the bound.
A program may use at most 64 MiB of HBM per device.

v0:
```python
import functools

import jax
import jax.numpy as jnp
from jax import lax
from jax.experimental import pallas as pl
from jax.experimental.pallas import tpu as pltpu
from jax.sharding import PartitionSpec as P

ITERS = 6
MESH = pl.DeviceIdType.MESH

damp_fraction = 0.01
sub_width = 16


GROUPS = 16


def exchange(nd, nl, x_ref, o_ref, pbuf, sbuf, rbuf, sems, beside=None):
    psend, precv, ssend, srecv, gsend, grecv, fsend, frecv = sems
    dp = lax.axis_index("dp")
    label = lax.axis_index("label")
    core = lax.rem(dp, 2)
    chip = (dp // 2) * nl + label
    n = (nd // 2) * nl
    lanes = pbuf.shape[2]
    partner = (dp + 1 - 2 * core, label)

    def ahead(d):
        return lax.rem(chip + d, n)

    def behind(d):
        return lax.rem(chip + n - d, n)

    def device(j):
        return (2 * (j // nl) + core, lax.rem(j, nl))

    def place(half, j):
        q = half * n + j
        return (
            pl.ds(pl.multiple_of(lax.rem(q, GROUPS) * 8, 8), 8),
            pl.ds(pl.multiple_of((q // GROUPS) * lanes, 128), lanes),
        )

    def remote(src, dst, send, recv, to):
        return pltpu.make_async_remote_copy(
            src_ref=src, dst_ref=dst, send_sem=send, recv_sem=recv, device_id=to, device_id_type=MESH
        )

    def pair(d):
        return remote(x_ref.at[place(1 - core, ahead(d))], pbuf.at[d], psend.at[d], precv.at[d], partner)

    def scatter(d):
        return remote(sbuf.at[d], rbuf.at[d], ssend.at[d], srecv.at[d], device(ahead(d)))

    def gather(d):
        own = o_ref.at[place(core, chip)]
        return remote(own, own, gsend.at[d], grecv.at[d], device(ahead(d)))

    def gathered(d):
        ref = o_ref.at[place(core, behind(d))]
        return remote(ref, ref, gsend.at[d], grecv.at[d], device(behind(d)))

    def forward(d):
        ref = o_ref.at[place(core, behind(d))]
        return remote(ref, ref, fsend.at[d], frecv.at[d], partner)

    def forwarded(d):
        ref = o_ref.at[place(1 - core, behind(d))]
        return remote(ref, ref, fsend.at[d], frecv.at[d], partner)

    def each(low, body, high=n):
        def step(d, carry):
            body(d)
            return carry

        lax.fori_loop(low, high, step, 0)

    def greet():
        barrier = pltpu.get_barrier_semaphore()
        pl.semaphore_signal(barrier, inc=1, device_id=partner, device_id_type=MESH)
        each(1, lambda d: pl.semaphore_signal(barrier, inc=1, device_id=device(ahead(d)), device_id_type=MESH))
        pl.semaphore_wait(barrier, n)

    def run():
        each(1, lambda d: pair(d).start())
        pair(0).start()

        def send_sum(d):
            pair(d).wait_recv()
            sbuf[d] = x_ref[place(core, ahead(d))] + pbuf[d]
            scatter(d).start()

        each(1, send_sum)
        if beside is not None:
            each(1, lambda e: [c.start() for c in beside(remote, dp, label, e, 0)], nl)
        pair(0).wait_recv()

        def add(d, acc):
            scatter(d).wait_recv()
            return acc + rbuf[d]

        o_ref[place(core, chip)] = lax.fori_loop(1, n, add, x_ref[place(core, chip)] + pbuf[0])
        each(1, lambda d: gather(d).start())
        forward(0).start()

        def pass_on(d):
            gathered(d).wait_recv()
            forward(d).start()

        each(1, pass_on)
        each(0, lambda d: forwarded(d).wait_recv())
        if beside is not None:
            each(1, lambda e: [c.wait_recv() for c in beside(remote, dp, label, e, 1)], nl)
            each(1, lambda e: [c.wait_send() for c in beside(remote, dp, label, e, 0)], nl)
        each(0, lambda d: pair(d).wait_send())
        each(1, lambda d: scatter(d).wait_send())
        each(1, lambda d: gather(d).wait_send())
        each(0, lambda d: forward(d).wait_send())

    return greet, run


def piece_lanes(width, nd, nl):
    parts = nd * nl // GROUPS
    return -(-width // (parts * 128)) * 128


def exchange_scratch(lanes, nd, nl):
    n = nd // 2 * nl
    return [pltpu.VMEM((n, 8, lanes), jnp.float32)] * 3 + [pltpu.SemaphoreType.DMA((n,))] * 8


def first_kernel(nd, nl, x_ref, w_ref, m_ref, o_ref, wg_ref, mg_ref, pbuf, sbuf, rbuf, *sems):
    wsend, wrecv, msend, mrecv = sems[8:]
    own = m_ref.shape[1]

    def beside(remote, dp, label, e, arriving):
        to = lax.rem(label + (nl - e if arriving else e), nl)
        at = to if arriving else label
        cols = (slice(None), pl.ds(pl.multiple_of(at * own, 128), own))
        return (
            remote(w_ref, wg_ref.at[at], wsend.at[e], wrecv.at[e], (dp, to)),
            remote(m_ref, mg_ref.at[cols], msend.at[e], mrecv.at[e], (dp, to)),
        )

    greet, run = exchange(nd, nl, x_ref, o_ref, pbuf, sbuf, rbuf, sems[:8], beside)
    greet()
    label = lax.axis_index("label")
    wg_ref[label] = w_ref[...]
    mg_ref[:, pl.ds(pl.multiple_of(label * own, 128), own)] = m_ref[...]
    run()


def first_sum(x, w, mask, nd, nl):
    lanes = x.shape[1] // (nd * nl // GROUPS)
    vmem = pl.BlockSpec(memory_space=pltpu.VMEM)
    return pl.pallas_call(
        functools.partial(first_kernel, nd, nl),
        out_shape=(
            jax.ShapeDtypeStruct(x.shape, jnp.float32),
            jax.ShapeDtypeStruct((nl,) + w.shape, w.dtype),
            jax.ShapeDtypeStruct((mask.shape[0], mask.shape[1] * nl), mask.dtype),
        ),
        in_specs=[vmem] * 3,
        out_specs=(vmem,) * 3,
        scratch_shapes=exchange_scratch(lanes, nd, nl) + [pltpu.SemaphoreType.DMA((nl,))] * 4,
        compiler_params=pltpu.CompilerParams(collective_id=2, has_side_effects=True, vmem_limit_bytes=40 << 20),
        name="first_sum",
    )(x, w, mask)


def two_terms(x):
    high = x.astype(jnp.bfloat16)
    low = (x - high.astype(jnp.float32)).astype(jnp.bfloat16)
    return jnp.concatenate([high, low], axis=0)


def step_kernel(
    nd, nl, scale, c_ref, diag_ref, damp_ref, d_ref, s_ref, r_ref, rho_ref,
    dn_ref, sn_ref, rn_ref, rhon_ref, x_ref, o_ref, pbuf, sbuf, rbuf, *sems
):
    block, width = d_ref.shape
    greet, run = exchange(nd, nl, x_ref, o_ref, pbuf, sbuf, rbuf, sems)
    inner = lax.dot_general(
        two_terms(d_ref[...]), c_ref[...], (((1,), (1,)), ((), ())), preferred_element_type=jnp.float32
    )
    inner = two_terms(inner[:block] + inner[block:])
    tile = width // 3
    for begin in range(0, width, tile):
        cols = pl.ds(begin, tile)
        outer = jnp.dot(inner, c_ref[:, cols], preferred_element_type=jnp.float32)
        x_ref[:, cols] = outer[:block] + outer[block:]
    if x_ref.shape[1] > width:
        x_ref[:, width:] = jnp.zeros((block, x_ref.shape[1] - width), jnp.float32)
    greet()
    run()

    def update(g, carry):
        rows = pl.ds(pl.multiple_of(g * 8, 8), 8)
        direction = d_ref[rows, :]
        rho = rho_ref[rows, :]
        image = scale * o_ref[rows, :width] + damp_ref[...] * direction
        alpha = rho / jnp.sum(direction * image, axis=1, keepdims=True)
        sn_ref[rows, :] = s_ref[rows, :] + alpha * direction
        resid = r_ref[rows, :] - alpha * image
        precond = resid / diag_ref[...]
        fresh = jnp.sum(resid * precond, axis=1, keepdims=True)
        rn_ref[rows, :] = resid
        dn_ref[rows, :] = precond + fresh / rho * direction
        rhon_ref[rows, :] = fresh
        return carry

    lax.fori_loop(0, block // 8, update, 0)


def one_step(calib, diag, damping, state, scale, nd, nl):
    block, width = state[0].shape
    lanes = piece_lanes(width + block, nd, nl)
    padded = (block, lanes * (nd * nl // GROUPS))
    vmem = pl.BlockSpec(memory_space=pltpu.VMEM)
    return pl.pallas_call(
        functools.partial(step_kernel, nd, nl, scale),
        out_shape=tuple(jax.ShapeDtypeStruct(x.shape, jnp.float32) for x in state),
        in_specs=[vmem] * 7,
        out_specs=(vmem,) * 4,
        scratch_shapes=[pltpu.VMEM(padded, jnp.float32)] * 2 + exchange_scratch(lanes, nd, nl),
        compiler_params=pltpu.CompilerParams(collective_id=0, has_side_effects=True, vmem_limit_bytes=48 << 20),
        name="one_step",
    )(calib, diag, damping, *state)


def small_kernel(nd, nl, x_ref, o_ref, buf, send, recv):
    n = nd * nl
    me = lax.axis_index("dp") * nl + lax.axis_index("label")

    def device(j):
        return (j // nl, lax.rem(j, nl))

    def out(d):
        return pltpu.make_async_remote_copy(
            src_ref=x_ref,
            dst_ref=buf.at[me],
            send_sem=send.at[d],
            recv_sem=recv.at[d],
            device_id=device(lax.rem(me + d, n)),
            device_id_type=MESH,
        )

    def arrived(d):
        j = lax.rem(me + n - d, n)
        return pltpu.make_async_remote_copy(
            src_ref=x_ref,
            dst_ref=buf.at[j],
            send_sem=send.at[d],
            recv_sem=recv.at[d],
            device_id=device(j),
            device_id_type=MESH,
        )

    def each(body):
        def step(d, carry):
            body(d)
            return carry

        lax.fori_loop(1, n, step, 0)

    barrier = pltpu.get_barrier_semaphore()
    each(lambda d: pl.semaphore_signal(barrier, inc=1, device_id=device(lax.rem(me + d, n)), device_id_type=MESH))
    pl.semaphore_wait(barrier, n - 1)
    each(lambda d: out(d).start())
    buf[me] = x_ref[...]
    each(lambda d: arrived(d).wait_recv())
    o_ref[...] = lax.fori_loop(1, n, lambda j, acc: acc + buf[j], buf[0])
    each(lambda d: out(d).wait_send())


def small_sum(x, nd, nl):
    n = nd * nl
    return pl.pallas_call(
        functools.partial(small_kernel, nd, nl),
        out_shape=jax.ShapeDtypeStruct(x.shape, jnp.float32),
        in_specs=[pl.BlockSpec(memory_space=pltpu.VMEM)],
        out_specs=pl.BlockSpec(memory_space=pltpu.VMEM),
        scratch_shapes=[
            pltpu.VMEM((n,) + x.shape, jnp.float32),
            pltpu.SemaphoreType.DMA((n,)),
            pltpu.SemaphoreType.DMA((n,)),
        ],
        compiler_params=pltpu.CompilerParams(collective_id=1, has_side_effects=True),
        name="small_sum",
    )(x)


def prune_kernel(w_ref, m_ref, l_ref, kept_ref, err_ref):
    block = w_ref.shape[0]
    err_ref[...] = jnp.zeros_like(err_ref)
    for begin in range(0, block, sub_width):
        rows = pl.ds(begin, sub_width)
        window = w_ref[rows, :].astype(jnp.float32)
        chosen = m_ref[rows, :].astype(jnp.float32)
        factor = l_ref[rows, :]
        if begin:
            window = window - jnp.dot(
                factor, err_ref[...], precision=lax.Precision.HIGHEST, preferred_element_type=jnp.float32
            )
        for offset in range(sub_width):
            index = begin + offset
            column = factor[:, index : index + 1]
            inverse = 1.0 / factor[offset : offset + 1, index : index + 1]
            error = chosen[offset : offset + 1, :] * window[offset : offset + 1, :] * inverse
            err_ref[index : index + 1, :] = error
            window = window - column * error
        kept_ref[rows, :] = ((1.0 - chosen) * window).astype(kept_ref.dtype)


def prune_rows(weights, mask, lower):
    block, rows = weights.shape
    tile = min(rows, 2048)
    spec = pl.BlockSpec((block, tile), lambda i: (0, i))
    return pl.pallas_call(
        prune_kernel,
        grid=(rows // tile,),
        out_shape=(
            jax.ShapeDtypeStruct((block, rows), jnp.bfloat16),
            jax.ShapeDtypeStruct((block, rows), jnp.float32),
        ),
        in_specs=[spec, spec, pl.BlockSpec((block, block), lambda i: (0, 0))],
        out_specs=(spec, spec),
        compiler_params=pltpu.CompilerParams(vmem_limit_bytes=32 << 20),
        name="prune_rows",
    )(weights, mask, lower)


def per_device(calib, block_weight, rest_weight, prune_mask):
    tokens = calib.shape[0]
    width = calib.shape[1]
    block = prune_mask.shape[1]
    nd, nl = lax.axis_size("dp"), lax.axis_size("label")
    total = tokens * nd * nl
    stat_rows = width // block
    padded = piece_lanes(width + block, nd, nl) * (nd * nl // GROUPS)
    local_sq = jnp.sum(jnp.square(calib.astype(jnp.float32)), axis=0)
    first = lax.dot_general(
        calib[:, :block], calib, (((0,), (0,)), ((), ())), preferred_element_type=jnp.float32
    )
    stats = jnp.pad(local_sq.reshape(stat_rows, block), ((0, block - stat_rows), (0, padded - width - block)))
    summed, weights, mask = first_sum(
        jnp.concatenate([first, stats], axis=1), block_weight.T, prune_mask.T.astype(jnp.bfloat16), nd, nl
    )
    weights = weights.reshape(block, -1)
    colsq = summed[:stat_rows, width : width + block].reshape(1, width)
    damping = damp_fraction * 2.0 * jnp.sum(colsq) / (total * width)
    scale = 2.0 / total
    diag = scale * colsq + damping
    resid = jnp.eye(block, width, dtype=jnp.float32)
    precond = resid / diag
    direction = precond
    rho = jnp.sum(resid * precond, axis=1, keepdims=True)
    image = scale * (summed[:, :width] / diag[:, :block].T) + damping * direction
    alpha = rho / jnp.sum(direction * image, axis=1, keepdims=True)
    solution = alpha * direction
    resid = resid - alpha * image
    precond = resid / diag
    fresh = jnp.sum(resid * precond, axis=1, keepdims=True)
    direction = precond + fresh / rho * direction
    state = (direction, solution, resid, fresh)
    for step in range(1, ITERS - 1):
        state = one_step(calib, diag, damping.reshape(1, 1), state, scale, nd, nl)
    direction, solution, resid, rho = state
    inner = jnp.einsum(
        "bk,tk->bt", direction, calib, precision=lax.Precision.HIGHEST, preferred_element_type=jnp.float32
    )
    local = jnp.pad(jnp.sum(inner * inner, axis=1)[None, :], ((0, 7), (0, 0)))
    energy = scale * small_sum(local, nd, nl)[0] + damping * jnp.sum(direction * direction, axis=1)
    solution = solution + rho / energy[:, None] * direction
    top = 0.5 * (solution[:, :block] + solution[:, :block].T)
    lower = jnp.linalg.cholesky(top)
    kept, errors = prune_rows(weights, mask, lower)
    own = prune_mask.shape[0]
    label = lax.axis_index("label")
    pruned_block = lax.dynamic_slice_in_dim(kept, label * own, own, 1).T
    rest_cols = rest_weight.shape[1]
    owned = lax.dynamic_slice_in_dim(solution, block + label * rest_cols, rest_cols, 1)
    cross = jax.scipy.linalg.solve_triangular(lower, owned, lower=True)
    delta = lax.dot_general(
        errors,
        cross,
        (((0,), (0,)), ((), ())),
        precision=lax.Precision.HIGHEST,
        preferred_element_type=jnp.float32,
    )
    updated_rest = (rest_weight.astype(jnp.float32) - delta).astype(jnp.bfloat16)
    return (pruned_block, updated_rest)


def solution(mesh):
    return jax.shard_map(
        per_device,
        mesh=mesh,
        in_specs=(
            P(("dp", "label"), None),
            P("dp", "label"),
            P("dp", "label"),
            P(("dp", "label"), None),
        ),
        out_specs=(P(("dp", "label"), None), P("dp", "label")),
        check_vma=False,
    )
```

profile of v0, /device:TPU:0, one launch (start us, length us, event | category | flops | bytes accessed | tf_op | source)
XLA Modules:
  0.0 354.7 jit_solution(1939829878342795459)
XLA Ops:
  0.6 0.0 copy-start.9
  0.6 2.5 multiply_reduce_fusion
  3.1 0.1 copy-done.9
  3.2 0.6 fusion.4
  3.8 0.1 select_maximum_fusion.x_ref
  3.9 0.8 copy-done.13
  4.7 0.1 copy.15
  4.8 63.2 %first_sum.1 = (f32[128,2816]{1,0:T(8,128)S(1)}, bf16[8,16,2048]{2,1,0:T(8,128)(2,1)S(1)}, bf16[128,2048]{1,0:T(8,128)(2,1)S(1)}) custom-call(f32[128,2816]{1,0:T(8,128)S(1)} %select_maximum_fusion.x_ref, bf16[16,2048]{1,0:T(8,128)(2,1)S(1)} %bitcast.48, bf16[128,256]{1,0:T(8,128)(2,1)S(1)} %convert_bitcast_fusion.m_ref), custom_call_target="tpu_custom_call" | custom-call | tf_op jit(solution)/shard_map/first_sum/pallas_call | solution.py:159
  68.1 0.8 copy-done.6
  68.9 0.6 slice_reduce_fusion
  70.2 0.4 multiply_reduce_fusion.3
  70.6 1.6 multiply_reduce_fusion.2
  72.2 0.2 multiply_add_fusion.1.d_ref
  72.5 0.9 copy-done.10
  73.3 0.1 copy.16.rho_ref
  73.5 53.6 %one_step.4 = (f32[128,2688]{1,0:T(8,128)S(1)}, f32[128,2688]{1,0:T(8,128)S(1)}, f32[128,2688]{1,0:T(8,128)S(1)}, f32[128,1]{1,0:T(8,128)S(1)}) custom-call(bf16[512,2688]{1,0:T(8,128)(2,1)} %c_ref.7, f32[1,2688]{1,0:T(1,128)S(1)} %bitcast.44, f32[1,1]{1,0:T(1,128)} %bitcast.4.damp_ref, f32[128,2688]{1,0:T(8,128)S(1)} %multiply_add_fusion.1.d_ref, ...), custom_call_target="tpu_custom_call" | custom-call | tf_op jit(solution)/shard_map/one_step/pallas_call | solution.py:223
  127.1 1.1 copy-done.2
  128.2 1.1 copy-done.3
  129.3 53.1 %one_step.5 = (f32[128,2688]{1,0:T(8,128)S(1)}, f32[128,2688]{1,0:T(8,128)S(1)}, f32[128,2688]{1,0:T(8,128)S(1)}, f32[128,1]{1,0:T(8,128)S(1)}) custom-call(bf16[512,2688]{1,0:T(8,128)(2,1)} %c_ref.7, f32[1,2688]{1,0:T(1,128)S(1)} %bitcast.45, f32[1,1]{1,0:T(1,128)} %bitcast.4.damp_ref, f32[128,2688]{1,0:T(8,128)S(1)} %get-tuple-element.25.d_ref, ...), custom_call_target="tpu_custom_call" | custom-call | tf_op jit(solution)/shard_map/one_step/pallas_call | solution.py:223
  182.4 1.1 copy-done.4
  183.4 1.1 copy-done.5
  184.6 53.1 %one_step.6 = (f32[128,2688]{1,0:T(8,128)S(1)}, f32[128,2688]{1,0:T(8,128)S(1)}, f32[128,2688]{1,0:T(8,128)S(1)}, f32[128,1]{1,0:T(8,128)S(1)}) custom-call(bf16[512,2688]{1,0:T(8,128)(2,1)} %c_ref.7, f32[1,2688]{1,0:T(1,128)S(1)} %bitcast.46, f32[1,1]{1,0:T(1,128)} %bitcast.4.damp_ref, f32[128,2688]{1,0:T(8,128)S(1)} %get-tuple-element.29.d_ref, ...), custom_call_target="tpu_custom_call" | custom-call | tf_op jit(solution)/shard_map/one_step/pallas_call | solution.py:223
  237.6 1.1 copy-done
  238.7 1.1 copy-done.1
  239.8 54.2 %one_step.7 = (f32[128,2688]{1,0:T(8,128)S(1)}, f32[128,2688]{1,0:T(8,128)S(1)}, f32[128,2688]{1,0:T(8,128)}, f32[128,1]{1,0:T(8,128)S(1)}) custom-call(bf16[512,2688]{1,0:T(8,128)(2,1)} %c_ref.7, f32[1,2688]{1,0:T(1,128)S(1)} %bitcast.47, f32[1,1]{1,0:T(1,128)} %bitcast.4.damp_ref, f32[128,2688]{1,0:T(8,128)S(1)} %get-tuple-element.33.d_ref, ...), custom_call_target="tpu_custom_call" | custom-call | tf_op jit(solution)/shard_map/one_step/pallas_call | solution.py:223
  294.0 1.5 copy.20
  295.6 1.5 copy.19
  297.1 4.7 %fusion.1 = f32[128]{0:T(128)S(1)} fusion(f32[128,2688]{1,0:T(8,128)S(1)} %get-tuple-element.39, bf16[512,2688]{1,0:T(8,128)(2,1)} %c_ref.7), kind=kOutput, calls=%fused_computation.16 | convolution fusion | flops 2114060160 | bytes 4129280 | tf_op jit(solution)/shard_map/bk,tk->bt/dot_general | solution.py:372
  301.8 0.6 pad.9.x_ref
  302.4 13.2 %small_sum.1 = f32[8,128]{1,0:T(8,128)} custom-call(f32[8,128]{1,0:T(8,128)} %pad.9.x_ref), custom_call_target="tpu_custom_call" | custom-call | tf_op jit(solution)/shard_map/small_sum/pallas_call | solution.py:281
  315.6 0.7 multiply_bitcast_fusion.1
  316.3 0.1 copy.17
  316.4 0.2 multiply_reduce_fusion.1
  316.6 0.1 copy.18
  316.7 0.1 fusion.9
  316.9 1.5 multiply_add_fusion
  318.4 1.1 copy-done.12
  319.4 0.1 copy.21
  319.5 0.9 fusion.8
  320.4 0.1 copy.22
  320.6 11.7 %cholesky.18 = f32[128,128]{1,0:T(8,128)S(1)} custom-call(f32[128,128]{1,0:T(8,128)S(1)} %fusion.7), custom_call_target="Cholesky" | custom-call | tf_op jit(solution)/shard_map/jit(cholesky)/cholesky | solution.py:379
  332.3 0.6 compare_reduce_fusion
  332.9 0.7 select_bitcast_fusion
  333.6 4.5 %prune_rows.1 = (bf16[128,2048]{1,0:T(8,128)(2,1)S(1)}, f32[128,2048]{1,0:T(8,128)S(1)}) custom-call(bf16[128,2048]{1,0:T(8,128)(2,1)S(1)} %bitcast.42, bf16[128,2048]{1,0:T(8,128)(2,1)S(1)} %copy-done.7, f32[128,128]{1,0:T(8,128)S(1)} %get-tuple-element.49.l_ref), custom_call_target="tpu_custom_call" | custom-call | tf_op jit(solution)/shard_map/prune_rows/pallas_call | solution.py:322
  338.1 0.7 copy.23
  338.9 9.8 %custom-call.7 = f32[1,128,128]{1,2,0:T(8,128)S(1)} custom-call(f32[1,128,128]{2,1,0:T(8,128)S(1)} %get-tuple-element.48), custom_call_target="InvertDiagBlocksLowerTriangular" | custom-call | tf_op jit(solution)/shard_map/jit(_solve_triangular)/triangular_solve | solution.py:386
  348.7 1.3 fusion.2
  350.0 4.7 %fusion = bf16[2048,320]{0,1:T(8,128)(2,1)} fusion(f32[128,2048]{1,0:T(8,128)S(1)} %get-tuple-element.41, f32[128,320]{1,0:T(8,128)S(1)} %fusion.2, bf16[2048,320]{0,1:T(8,128)(2,1)} %param.6), kind=kOutput, calls=%fused_computation.2 | convolution fusion | flops 1008599040 | bytes 3833856 | tf_op jit(solution)/shard_map/dot_general | solution.py:387
  (27 shorter events, 0.2 us)
Async XLA Ops:
  0.6 2.6 copy-start.9
  3.8 0.9 copy-start.13
  3.8 1.0 copy-start.8
  68.1 0.8 copy-start.6
  72.2 1.1 copy-start.10
  127.1 1.1 copy-start.2
  128.2 1.1 copy-start.3
  182.4 1.1 copy-start.4
  183.4 1.1 copy-start.5
  237.6 1.1 copy-start
  238.7 1.1 copy-start.1
  301.8 15.1 %copy-start.11 = (f32[128,2688]{0,1:T(8,128)S(1)}, f32[128,2688]{0,1:T(8,128)}, u32[]{:S(2)}) copy-start(f32[128,2688]{0,1:T(8,128)} %copy.20) | copy-start | bytes 4128772
  318.3 1.1 copy-start.12
  319.4 14.2 %copy-start.7 = (bf16[128,2048]{1,0:T(8,128)(2,1)S(1)}, bf16[128,2048]{1,0:T(8,128)(2,1)}, u32[]{:S(2)}) copy-start(bf16[128,2048]{1,0:T(8,128)(2,1)} %copy-done.6) | copy-start | bytes 1572868
where the time goes:
time: 355 us
  Pallas kernels  295 us (83%)
  other arithmetic  31.7 us (9%)
  local copies, waits for them, and re-layouts  15.2 us (4%)
  matrix products  11.3 us (3%)
    pallas_call x4, Pallas kernels, one_step(): pl.pallas_call(functools.partial(step_kernel, nd, nl, scale), out_shape=t...  214 us
    pallas_call x1, Pallas kernels, first_sum(): pl.pallas_call(functools.partial(first_kernel, nd, nl), out_shape=(jax.Sh...  63.2 us
    pallas_call x1, Pallas kernels, small_sum(): pl.pallas_call(functools.partial(small_kernel, nd, nl), out_shape=jax.Sha...  13.2 us
    another operation x3, other arithmetic, per_device(): lower = jnp.linalg.cholesky(top)  12.4 us
    unnamed x31, local copies, waits for them, and re-layouts  11 us
    another operation x2, other arithmetic, per_device(): cross = jax.scipy.linalg.solve_triangular(lower, owned, lower=True)  10.5 us

commit v1 on v0

--- a/solution.py
+++ b/solution.py
@@ -177,25 +177,26 @@
     return jnp.concatenate([high, low], axis=0)
 
 
-def step_kernel(
-    nd, nl, scale, c_ref, diag_ref, damp_ref, d_ref, s_ref, r_ref, rho_ref,
-    dn_ref, sn_ref, rn_ref, rhon_ref, x_ref, o_ref, pbuf, sbuf, rbuf, *sems
+def steps_kernel(
+    nd, nl, scale, steps, c_ref, diag_ref, damp_ref, d0_ref, s0_ref, r0_ref, rho0_ref,
+    d_ref, s_ref, rho_ref, local_ref, r_ref, x_ref, o_ref, pbuf, sbuf, rbuf, *sems
 ):
     block, width = d_ref.shape
     greet, run = exchange(nd, nl, x_ref, o_ref, pbuf, sbuf, rbuf, sems)
-    inner = lax.dot_general(
-        two_terms(d_ref[...]), c_ref[...], (((1,), (1,)), ((), ())), preferred_element_type=jnp.float32
-    )
-    inner = two_terms(inner[:block] + inner[block:])
-    tile = width // 3
-    for begin in range(0, width, tile):
-        cols = pl.ds(begin, tile)
-        outer = jnp.dot(inner, c_ref[:, cols], preferred_element_type=jnp.float32)
-        x_ref[:, cols] = outer[:block] + outer[block:]
+    d_ref[...] = d0_ref[...]
+    s_ref[...] = s0_ref[...]
+    r_ref[...] = r0_ref[...]
+    rho_ref[...] = rho0_ref[...]
     if x_ref.shape[1] > width:
         x_ref[:, width:] = jnp.zeros((block, x_ref.shape[1] - width), jnp.float32)
+    tile = width // 3
     greet()
-    run()
+
+    def project():
+        inner = lax.dot_general(
+            two_terms(d_ref[...]), c_ref[...], (((1,), (1,)), ((), ())), preferred_element_type=jnp.float32
+        )
+        return inner[:block] + inner[block:]
 
     def update(g, carry):
         rows = pl.ds(pl.multiple_of(g * 8, 8), 8)
@@ -203,31 +204,57 @@
         rho = rho_ref[rows, :]
         image = scale * o_ref[rows, :width] + damp_ref[...] * direction
         alpha = rho / jnp.sum(direction * image, axis=1, keepdims=True)
-        sn_ref[rows, :] = s_ref[rows, :] + alpha * direction
+        s_ref[rows, :] = s_ref[rows, :] + alpha * direction
         resid = r_ref[rows, :] - alpha * image
         precond = resid / diag_ref[...]
         fresh = jnp.sum(resid * precond, axis=1, keepdims=True)
-        rn_ref[rows, :] = resid
-        dn_ref[rows, :] = precond + fresh / rho * direction
-        rhon_ref[rows, :] = fresh
+        r_ref[rows, :] = resid
+        d_ref[rows, :] = precond + fresh / rho * direction
+        rho_ref[rows, :] = fresh
         return carry
 
-    lax.fori_loop(0, block // 8, update, 0)
-
-
-def one_step(calib, diag, damping, state, scale, nd, nl):
+    def step(index, carry):
+        inner = two_terms(project())
+        for begin in range(0, width, tile):
+            cols = pl.ds(begin, tile)
+            outer = jnp.dot(inner, c_ref[:, cols], preferred_element_type=jnp.float32)
+            x_ref[:, cols] = outer[:block] + outer[block:]
+        run()
+        lax.fori_loop(0, block // 8, update, 0)
+        return carry
+
+    lax.fori_loop(0, steps, step, 0)
+    inner = project()
+    local_ref[...] = lax.dot_general(
+        jnp.ones((8, inner.shape[1]), jnp.float32),
+        inner * inner,
+        (((1,), (1,)), ((), ())),
+        precision=lax.Precision.HIGHEST,
+        preferred_element_type=jnp.float32,
+    )
+
+
+def middle_steps(calib, diag, damping, state, scale, steps, nd, nl):
     block, width = state[0].shape
     lanes = piece_lanes(width + block, nd, nl)
     padded = (block, lanes * (nd * nl // GROUPS))
     vmem = pl.BlockSpec(memory_space=pltpu.VMEM)
+    whole = jax.ShapeDtypeStruct((block, width), jnp.float32)
     return pl.pallas_call(
-        functools.partial(step_kernel, nd, nl, scale),
-        out_shape=tuple(jax.ShapeDtypeStruct(x.shape, jnp.float32) for x in state),
+        functools.partial(steps_kernel, nd, nl, scale, steps),
+        out_shape=(
+            whole,
+            whole,
+            jax.ShapeDtypeStruct((block, 1), jnp.float32),
+            jax.ShapeDtypeStruct((8, block), jnp.float32),
+        ),
         in_specs=[vmem] * 7,
         out_specs=(vmem,) * 4,
-        scratch_shapes=[pltpu.VMEM(padded, jnp.float32)] * 2 + exchange_scratch(lanes, nd, nl),
-        compiler_params=pltpu.CompilerParams(collective_id=0, has_side_effects=True, vmem_limit_bytes=48 << 20),
-        name="one_step",
+        scratch_shapes=[pltpu.VMEM((block, width), jnp.float32)]
+        + [pltpu.VMEM(padded, jnp.float32)] * 2
+        + exchange_scratch(lanes, nd, nl),
+        compiler_params=pltpu.CompilerParams(collective_id=0, has_side_effects=True, vmem_limit_bytes=52 << 20),
+        name="middle_steps",
     )(calib, diag, damping, *state)
 
 
@@ -293,44 +320,55 @@
     )(x)
 
 
-def prune_kernel(w_ref, m_ref, l_ref, kept_ref, err_ref):
+def prune_kernel(w_ref, m_ref, l_ref, t_ref, kept_ref, err_ref, cross_ref):
     block = w_ref.shape[0]
     err_ref[...] = jnp.zeros_like(err_ref)
+    cross_ref[...] = jnp.zeros_like(cross_ref)
+
+    def earlier(factor, ref):
+        return jnp.dot(factor, ref[...], precision=lax.Precision.HIGHEST, preferred_element_type=jnp.float32)
+
     for begin in range(0, block, sub_width):
         rows = pl.ds(begin, sub_width)
         window = w_ref[rows, :].astype(jnp.float32)
+        target = t_ref[rows, :]
         chosen = m_ref[rows, :].astype(jnp.float32)
         factor = l_ref[rows, :]
         if begin:
-            window = window - jnp.dot(
-                factor, err_ref[...], precision=lax.Precision.HIGHEST, preferred_element_type=jnp.float32
-            )
+            window = window - earlier(factor, err_ref)
+            target = target - earlier(factor, cross_ref)
         for offset in range(sub_width):
             index = begin + offset
+            one = slice(offset, offset + 1)
             column = factor[:, index : index + 1]
-            inverse = 1.0 / factor[offset : offset + 1, index : index + 1]
-            error = chosen[offset : offset + 1, :] * window[offset : offset + 1, :] * inverse
+            inverse = 1.0 / factor[one, index : index + 1]
+            error = chosen[one, :] * window[one, :] * inverse
+            solved = target[one, :] * inverse
             err_ref[index : index + 1, :] = error
+            cross_ref[index : index + 1, :] = solved
             window = window - column * error
+            target = target - column * solved
         kept_ref[rows, :] = ((1.0 - chosen) * window).astype(kept_ref.dtype)
 
 
-def prune_rows(weights, mask, lower):
+def prune_rows(weights, mask, lower, target):
     block, rows = weights.shape
     tile = min(rows, 2048)
     spec = pl.BlockSpec((block, tile), lambda i: (0, i))
+    fixed = [pl.BlockSpec(x.shape, lambda i: (0, 0)) for x in (lower, target)]
     return pl.pallas_call(
         prune_kernel,
         grid=(rows // tile,),
         out_shape=(
             jax.ShapeDtypeStruct((block, rows), jnp.bfloat16),
             jax.ShapeDtypeStruct((block, rows), jnp.float32),
+            jax.ShapeDtypeStruct(target.shape, jnp.float32),
         ),
-        in_specs=[spec, spec, pl.BlockSpec((block, block), lambda i: (0, 0))],
-        out_specs=(spec, spec),
+        in_specs=[spec, spec] + fixed,
+        out_specs=(spec, spec, fixed[1]),
         compiler_params=pltpu.CompilerParams(vmem_limit_bytes=32 << 20),
         name="prune_rows",
-    )(weights, mask, lower)
+    )(weights, mask, lower, target)
 
 
 def per_device(calib, block_weight, rest_weight, prune_mask):
@@ -366,24 +404,19 @@
     fresh = jnp.sum(resid * precond, axis=1, keepdims=True)
     direction = precond + fresh / rho * direction
     state = (direction, solution, resid, fresh)
-    for step in range(1, ITERS - 1):
-        state = one_step(calib, diag, damping.reshape(1, 1), state, scale, nd, nl)
-    direction, solution, resid, rho = state
-    inner = jnp.einsum(
-        "bk,tk->bt", direction, calib, precision=lax.Precision.HIGHEST, preferred_element_type=jnp.float32
-    )
-    local = jnp.pad(jnp.sum(inner * inner, axis=1)[None, :], ((0, 7), (0, 0)))
+    direction, solution, rho, local = middle_steps(
+        calib, diag, damping.reshape(1, 1), state, scale, ITERS - 2, nd, nl
+    )
     energy = scale * small_sum(local, nd, nl)[0] + damping * jnp.sum(direction * direction, axis=1)
     solution = solution + rho / energy[:, None] * direction
     top = 0.5 * (solution[:, :block] + solution[:, :block].T)
     lower = jnp.linalg.cholesky(top)
-    kept, errors = prune_rows(weights, mask, lower)
     own = prune_mask.shape[0]
     label = lax.axis_index("label")
-    pruned_block = lax.dynamic_slice_in_dim(kept, label * own, own, 1).T
     rest_cols = rest_weight.shape[1]
     owned = lax.dynamic_slice_in_dim(solution, block + label * rest_cols, rest_cols, 1)
-    cross = jax.scipy.linalg.solve_triangular(lower, owned, lower=True)
+    kept, errors, cross = prune_rows(weights, mask, lower, owned)
+    pruned_block = lax.dynamic_slice_in_dim(kept, label * own, own, 1).T
     delta = lax.dot_general(
         errors,
         cross,

time: 355 us -> 305 us (0.86)
  Pallas kernels: 295 us -> 271 us
  local copies, waits for them, and re-layouts: 15.2 us -> 4.73 us
  other arithmetic: 31.7 us -> 22.4 us
  matrix products: 11.3 us -> 5.24 us
    pallas_call x4 -> x1, Pallas kernels: 214 us -> 190 us  [middle_steps(): pl.pallas_call(functools.partial(steps_kernel, nd, nl, scale, steps), out...]
    another operation x2 -> x0, other arithmetic: 10.5 us -> none  [per_device(): cross = jax.scipy.linalg.solve_triangular(lower, owned, lower=True)]
    unnamed x31 -> x19, local copies, waits for them, and re-layouts: 11 us -> 3.12 us
    dot_general x1 -> x0, matrix products: 4.68 us -> none  [per_device(): jnp.einsum('bk,tk->bt', direction, calib, precision=lax.Precision.HIGHEST...]
where the time goes in v1:
time: 305 us; the launch traced here: 304 us
  Pallas kernels  271 us (89%)
  other arithmetic  22.4 us (7%)
  matrix products  5.24 us (2%)
  local copies, waits for them, and re-layouts  4.73 us (2%)
    pallas_call x1, Pallas kernels, middle_steps(): pl.pallas_call(functools.partial(steps_kernel, nd, nl, scale, steps), out...  190 us
    pallas_call x1, Pallas kernels, first_sum(): pl.pallas_call(functools.partial(first_kernel, nd, nl), out_shape=(jax.Sh...  63.2 us
    another operation x3, other arithmetic, per_device(): lower = jnp.linalg.cholesky(top)  12.4 us
    pallas_call x1, Pallas kernels, small_sum(): pl.pallas_call(functools.partial(small_kernel, nd, nl), out_shape=jax.Sha...  12.2 us

profile of v1, /device:TPU:0, one launch (start us, length us, event | category | flops | bytes accessed | tf_op | source)
XLA Modules:
  0.0 304.5 jit_solution(1209218565321712171)
XLA Ops:
  0.6 0.0 copy-start.4
  0.6 2.5 multiply_reduce_fusion
  3.1 0.1 copy-done.4
  3.2 0.6 fusion.1
  3.8 0.0 copy-start.7
  3.8 0.0 copy-start.2
  3.8 0.1 select_maximum_fusion.x_ref
  3.9 0.8 copy-done.7
  4.7 0.1 copy.13
  4.8 0.0 copy-done.2
  4.8 63.2 %first_sum.1 = (f32[128,2816]{1,0:T(8,128)S(1)}, bf16[8,16,2048]{2,1,0:T(8,128)(2,1)S(1)}, bf16[128,2048]{1,0:T(8,128)(2,1)S(1)}) custom-call(f32[128,2816]{1,0:T(8,128)S(1)} %select_maximum_fusion.x_ref, bf16[16,2048]{1,0:T(8,128)(2,1)S(1)} %bitcast.35, bf16[128,256]{1,0:T(8,128)(2,1)S(1)} %convert_bitcast_fusion.m_ref), custom_call_target="tpu_custom_call" | custom-call | tf_op jit(solution)/shard_map/first_sum/pallas_call | solution.py:159
  68.1 0.0 copy-start
  68.1 0.8 copy-done
  68.9 0.6 slice_reduce_fusion
  70.2 0.4 multiply_reduce_fusion.3
  70.6 1.7 multiply_reduce_fusion.2
  72.3 0.0 copy-start.5
  72.3 1.5 multiply_add_fusion.1.d0_ref
  73.8 0.0 copy-done.5
  73.8 0.1 copy.14.rho0_ref
  73.9 189.8 %middle_steps.1 = (f32[128,2688]{1,0:T(8,128)S(1)}, f32[128,2688]{1,0:T(8,128)}, f32[128,1]{1,0:T(8,128)S(1)}, f32[8,128]{1,0:T(8,128)S(1)}) custom-call(bf16[512,2688]{1,0:T(8,128)(2,1)} %c_ref.1, f32[1,2688]{1,0:T(1,128)S(1)} %bitcast.37, f32[1,1]{1,0:T(1,128)} %bitcast.4.damp_ref, f32[128,2688]{1,0:T(8,128)} %multiply_add_fusion.1.d0_ref, ...), custom_call_target="tpu_custom_call" | custom-call | tf_op jit(solution)/shard_map/middle_steps/pallas_call | solution.py:243
  263.7 0.0 copy-start.3
  263.8 0.6 copy-done.3
  264.3 12.2 %small_sum.1 = f32[8,128]{1,0:T(8,128)} custom-call(f32[8,128]{1,0:T(8,128)} %copy-done.3), custom_call_target="tpu_custom_call" | custom-call | tf_op jit(solution)/shard_map/small_sum/pallas_call | solution.py:308
  276.6 0.7 multiply_bitcast_fusion.1
  277.3 0.1 copy.15
  277.4 0.2 multiply_reduce_fusion.1
  277.6 0.1 copy.16
  277.7 0.1 fusion.5
  277.8 1.5 multiply_add_fusion
  279.3 0.0 copy-start.6
  279.4 0.0 copy-start.1
  279.4 0.1 copy.17
  279.5 0.1 copy.18
  279.6 11.7 %cholesky.18 = f32[128,128]{1,0:T(8,128)S(1)} custom-call(f32[128,128]{1,0:T(8,128)S(1)} %fusion.3), custom_call_target="Cholesky" | custom-call | tf_op jit(solution)/shard_map/jit(cholesky)/cholesky | solution.py:413
  291.4 0.0 copy-done.6
  291.4 0.6 compare_reduce_fusion
  292.0 0.7 select_select_fusion.l_ref
  292.7 1.1 constant_dynamic-slice_fusion.t_ref
  293.7 0.0 copy-done.1
  293.8 5.3 %prune_rows.1 = (bf16[128,2048]{1,0:T(8,128)(2,1)S(1)}, f32[128,2048]{1,0:T(8,128)S(1)}, f32[128,320]{1,0:T(8,128)S(1)}) custom-call(bf16[128,2048]{1,0:T(8,128)(2,1)S(1)} %bitcast.34, bf16[128,2048]{1,0:T(8,128)(2,1)S(1)} %copy-done.1, f32[128,128]{1,0:T(8,128)S(1)} %select_select_fusion.l_ref, f32[128,320]{1,0:T(8,128)S(1)} %constant_dynamic-slice_fusion.t_ref), custom_call_target="tpu_custom_call" | custom-call | tf_op jit(solution)/shard_map/prune_rows/pallas_call | solution.py:359
  299.1 0.7 copy.19
  299.8 4.7 %fusion = bf16[2048,320]{0,1:T(8,128)(2,1)} fusion(f32[128,2048]{1,0:T(8,128)S(1)} %get-tuple-element.20, f32[128,320]{1,0:T(8,128)S(1)} %get-tuple-element.21, bf16[2048,320]{0,1:T(8,128)(2,1)} %param.6), kind=kOutput, calls=%fused_computation.2 | convolution fusion | flops 1008599040 | bytes 3833856 | tf_op jit(solution)/shard_map/dot_general | solution.py:420
  (12 shorter events, 0.1 us)
Async XLA Ops:
  0.6 2.6 copy-start.4
  3.8 0.9 copy-start.7
  3.8 1.0 copy-start.2
  68.1 0.8 copy-start
  72.3 1.5 copy-start.5
  263.7 0.6 copy-start.3
  279.3 12.0 %copy-start.6 = (f32[128,2688]{1,0:T(8,128)}, f32[128,2688]{1,0:T(8,128)S(1)}, u32[]{:S(2)}) copy-start(f32[128,2688]{1,0:T(8,128)S(1)} %multiply_add_fusion) | copy-start | bytes 4128772
  279.4 14.4 %copy-start.1 = (bf16[128,2048]{1,0:T(8,128)(2,1)S(1)}, bf16[128,2048]{1,0:T(8,128)(2,1)}, u32[]{:S(2)}) copy-start(bf16[128,2048]{1,0:T(8,128)(2,1)} %copy-done) | copy-start | bytes 1572868

commit v2 on v1

--- a/solution.py
+++ b/solution.py
@@ -17,7 +17,7 @@
 GROUPS = 16
 
 
-def exchange(nd, nl, x_ref, o_ref, pbuf, sbuf, rbuf, sems, beside=None):
+def exchange(nd, nl, x_ref, o_ref, pbuf, sbuf, rbuf, sems):
     psend, precv, ssend, srecv, gsend, grecv, fsend, frecv = sems
     dp = lax.axis_index("dp")
     label = lax.axis_index("label")
@@ -93,8 +93,6 @@
             scatter(d).start()
 
         each(1, send_sum)
-        if beside is not None:
-            each(1, lambda e: [c.start() for c in beside(remote, dp, label, e, 0)], nl)
         pair(0).wait_recv()
 
         def add(d, acc):
@@ -111,15 +109,28 @@
 
         each(1, pass_on)
         each(0, lambda d: forwarded(d).wait_recv())
-        if beside is not None:
-            each(1, lambda e: [c.wait_recv() for c in beside(remote, dp, label, e, 1)], nl)
-            each(1, lambda e: [c.wait_send() for c in beside(remote, dp, label, e, 0)], nl)
         each(0, lambda d: pair(d).wait_send())
         each(1, lambda d: scatter(d).wait_send())
         each(1, lambda d: gather(d).wait_send())
         each(0, lambda d: forward(d).wait_send())
 
-    return greet, run
+    def energy(local_ref, part, slots, sums):
+        esend, erecv, csend, crecv = sums
+        near = remote(local_ref, part, esend, erecv, partner)
+        near.start()
+        near.wait_recv()
+        slots[chip] = local_ref[...] + part[...]
+
+        def far(d, j):
+            return remote(slots.at[j], slots.at[j], csend.at[d], crecv.at[d], device(ahead(d)))
+
+        each(1, lambda d: far(d, chip).start())
+        each(1, lambda d: far(d, behind(d)).wait_recv())
+        near.wait_send()
+        each(1, lambda d: far(d, chip).wait_send())
+        return lax.fori_loop(1, n, lambda j, acc: acc + slots[j], slots[0])
+
+    return greet, run, energy, remote, each
 
 
 def piece_lanes(width, nd, nl):
@@ -132,43 +143,24 @@
     return [pltpu.VMEM((n, 8, lanes), jnp.float32)] * 3 + [pltpu.SemaphoreType.DMA((n,))] * 8
 
 
-def first_kernel(nd, nl, x_ref, w_ref, m_ref, o_ref, wg_ref, mg_ref, pbuf, sbuf, rbuf, *sems):
-    wsend, wrecv, msend, mrecv = sems[8:]
-    own = m_ref.shape[1]
-
-    def beside(remote, dp, label, e, arriving):
-        to = lax.rem(label + (nl - e if arriving else e), nl)
-        at = to if arriving else label
-        cols = (slice(None), pl.ds(pl.multiple_of(at * own, 128), own))
-        return (
-            remote(w_ref, wg_ref.at[at], wsend.at[e], wrecv.at[e], (dp, to)),
-            remote(m_ref, mg_ref.at[cols], msend.at[e], mrecv.at[e], (dp, to)),
-        )
-
-    greet, run = exchange(nd, nl, x_ref, o_ref, pbuf, sbuf, rbuf, sems[:8], beside)
+def first_kernel(nd, nl, x_ref, o_ref, pbuf, sbuf, rbuf, *sems):
+    greet, run = exchange(nd, nl, x_ref, o_ref, pbuf, sbuf, rbuf, sems)[:2]
     greet()
-    label = lax.axis_index("label")
-    wg_ref[label] = w_ref[...]
-    mg_ref[:, pl.ds(pl.multiple_of(label * own, 128), own)] = m_ref[...]
     run()
 
 
-def first_sum(x, w, mask, nd, nl):
+def first_sum(x, nd, nl):
     lanes = x.shape[1] // (nd * nl // GROUPS)
     vmem = pl.BlockSpec(memory_space=pltpu.VMEM)
     return pl.pallas_call(
         functools.partial(first_kernel, nd, nl),
-        out_shape=(
-            jax.ShapeDtypeStruct(x.shape, jnp.float32),
-            jax.ShapeDtypeStruct((nl,) + w.shape, w.dtype),
-            jax.ShapeDtypeStruct((mask.shape[0], mask.shape[1] * nl), mask.dtype),
-        ),
-        in_specs=[vmem] * 3,
-        out_specs=(vmem,) * 3,
-        scratch_shapes=exchange_scratch(lanes, nd, nl) + [pltpu.SemaphoreType.DMA((nl,))] * 4,
+        out_shape=jax.ShapeDtypeStruct(x.shape, jnp.float32),
+        in_specs=[vmem],
+        out_specs=vmem,
+        scratch_shapes=exchange_scratch(lanes, nd, nl),
         compiler_params=pltpu.CompilerParams(collective_id=2, has_side_effects=True, vmem_limit_bytes=40 << 20),
         name="first_sum",
-    )(x, w, mask)
+    )(x)
 
 
 def two_terms(x):
@@ -178,11 +170,31 @@
 
 
 def steps_kernel(
-    nd, nl, scale, steps, c_ref, diag_ref, damp_ref, d0_ref, s0_ref, r0_ref, rho0_ref,
-    d_ref, s_ref, rho_ref, local_ref, r_ref, x_ref, o_ref, pbuf, sbuf, rbuf, *sems
+    nd, nl, scale, steps, c_ref, diag_ref, damp_ref, d0_ref, s0_ref, r0_ref, rho0_ref, w_ref, m_ref,
+    d_ref, s_ref, rho_ref, energy_ref, wg_ref, mg_ref, r_ref, local_ref, part, slots, x_ref, o_ref,
+    pbuf, sbuf, rbuf, *sems
 ):
     block, width = d_ref.shape
-    greet, run = exchange(nd, nl, x_ref, o_ref, pbuf, sbuf, rbuf, sems)
+    greet, run, energy, remote, each = exchange(nd, nl, x_ref, o_ref, pbuf, sbuf, rbuf, sems[:8])
+    wsend, wrecv, msend, mrecv = sems[8:12]
+    dp = lax.axis_index("dp")
+    label = lax.axis_index("label")
+    own = m_ref.shape[1]
+    share = -(-(nl - 1) // steps)
+
+    def columns(at):
+        return (slice(None), pl.ds(pl.multiple_of(at * own, 128), own))
+
+    def beside(e, arriving):
+        to = lax.rem(label + (nl - e if arriving else e), nl)
+        at = to if arriving else label
+        return (
+            remote(w_ref, wg_ref.at[at], wsend.at[e], wrecv.at[e], (dp, to)),
+            remote(m_ref, mg_ref.at[columns(at)], msend.at[e], mrecv.at[e], (dp, to)),
+        )
+
+    wg_ref[label] = w_ref[...]
+    mg_ref[columns(label)] = m_ref[...]
     d_ref[...] = d0_ref[...]
     s_ref[...] = s0_ref[...]
     r_ref[...] = r0_ref[...]
@@ -214,6 +226,14 @@
         return carry
 
     def step(index, carry):
+        first = 1 + index * share
+
+        def send(e, carry):
+            for copy in beside(e, False):
+                copy.start()
+            return carry
+
+        lax.fori_loop(first, jnp.minimum(first + share, nl), send, 0)
         inner = two_terms(project())
         for begin in range(0, width, tile):
             cols = pl.ds(begin, tile)
@@ -232,11 +252,15 @@
         precision=lax.Precision.HIGHEST,
         preferred_element_type=jnp.float32,
     )
-
-
-def middle_steps(calib, diag, damping, state, scale, steps, nd, nl):
+    energy_ref[...] = energy(local_ref, part, slots, sems[12:])
+    each(1, lambda e: [copy.wait_recv() for copy in beside(e, True)], nl)
+    each(1, lambda e: [copy.wait_send() for copy in beside(e, False)], nl)
+
+
+def middle_steps(calib, diag, damping, state, w, mask, scale, steps, nd, nl):
     block, width = state[0].shape
     lanes = piece_lanes(width + block, nd, nl)
+    n = nd // 2 * nl
     padded = (block, lanes * (nd * nl // GROUPS))
     vmem = pl.BlockSpec(memory_space=pltpu.VMEM)
     whole = jax.ShapeDtypeStruct((block, width), jnp.float32)
@@ -247,77 +271,22 @@
             whole,
             jax.ShapeDtypeStruct((block, 1), jnp.float32),
             jax.ShapeDtypeStruct((8, block), jnp.float32),
+            jax.ShapeDtypeStruct((nl,) + w.shape, w.dtype),
+            jax.ShapeDtypeStruct((mask.shape[0], mask.shape[1] * nl), mask.dtype),
         ),
-        in_specs=[vmem] * 7,
-        out_specs=(vmem,) * 4,
+        in_specs=[vmem] * 9,
+        out_specs=(vmem,) * 6,
         scratch_shapes=[pltpu.VMEM((block, width), jnp.float32)]
+        + [pltpu.VMEM((8, block), jnp.float32)] * 2
+        + [pltpu.VMEM((n, 8, block), jnp.float32)]
         + [pltpu.VMEM(padded, jnp.float32)] * 2
-        + exchange_scratch(lanes, nd, nl),
+        + exchange_scratch(lanes, nd, nl)
+        + [pltpu.SemaphoreType.DMA((nl,))] * 4
+        + [pltpu.SemaphoreType.DMA] * 2
+        + [pltpu.SemaphoreType.DMA((n,))] * 2,
         compiler_params=pltpu.CompilerParams(collective_id=0, has_side_effects=True, vmem_limit_bytes=52 << 20),
         name="middle_steps",
-    )(calib, diag, damping, *state)
-
-
-def small_kernel(nd, nl, x_ref, o_ref, buf, send, recv):
-    n = nd * nl
-    me = lax.axis_index("dp") * nl + lax.axis_index("label")
-
-    def device(j):
-        return (j // nl, lax.rem(j, nl))
-
-    def out(d):
-        return pltpu.make_async_remote_copy(
-            src_ref=x_ref,
-            dst_ref=buf.at[me],
-            send_sem=send.at[d],
-            recv_sem=recv.at[d],
-            device_id=device(lax.rem(me + d, n)),
-            device_id_type=MESH,
-        )
-
-    def arrived(d):
-        j = lax.rem(me + n - d, n)
-        return pltpu.make_async_remote_copy(
-            src_ref=x_ref,
-            dst_ref=buf.at[j],
-            send_sem=send.at[d],
-            recv_sem=recv.at[d],
-            device_id=device(j),
-            device_id_type=MESH,
-        )
-
-    def each(body):
-        def step(d, carry):
-            body(d)
-            return carry
-
-        lax.fori_loop(1, n, step, 0)
-
-    barrier = pltpu.get_barrier_semaphore()
-    each(lambda d: pl.semaphore_signal(barrier, inc=1, device_id=device(lax.rem(me + d, n)), device_id_type=MESH))
-    pl.semaphore_wait(barrier, n - 1)
-    each(lambda d: out(d).start())
-    buf[me] = x_ref[...]
-    each(lambda d: arrived(d).wait_recv())
-    o_ref[...] = lax.fori_loop(1, n, lambda j, acc: acc + buf[j], buf[0])
-    each(lambda d: out(d).wait_send())
-
-
-def small_sum(x, nd, nl):
-    n = nd * nl
-    return pl.pallas_call(
-        functools.partial(small_kernel, nd, nl),
-        out_shape=jax.ShapeDtypeStruct(x.shape, jnp.float32),
-        in_specs=[pl.BlockSpec(memory_space=pltpu.VMEM)],
-        out_specs=pl.BlockSpec(memory_space=pltpu.VMEM),
-        scratch_shapes=[
-            pltpu.VMEM((n,) + x.shape, jnp.float32),
-            pltpu.SemaphoreType.DMA((n,)),
-            pltpu.SemaphoreType.DMA((n,)),
-        ],
-        compiler_params=pltpu.CompilerParams(collective_id=1, has_side_effects=True),
-        name="small_sum",
-    )(x)
+    )(calib, diag, damping, *state, w, mask)
 
 
 def prune_kernel(w_ref, m_ref, l_ref, t_ref, kept_ref, err_ref, cross_ref):
@@ -384,10 +353,7 @@
         calib[:, :block], calib, (((0,), (0,)), ((), ())), preferred_element_type=jnp.float32
     )
     stats = jnp.pad(local_sq.reshape(stat_rows, block), ((0, block - stat_rows), (0, padded - width - block)))
-    summed, weights, mask = first_sum(
-        jnp.concatenate([first, stats], axis=1), block_weight.T, prune_mask.T.astype(jnp.bfloat16), nd, nl
-    )
-    weights = weights.reshape(block, -1)
+    summed = first_sum(jnp.concatenate([first, stats], axis=1), nd, nl)
     colsq = summed[:stat_rows, width : width + block].reshape(1, width)
     damping = damp_fraction * 2.0 * jnp.sum(colsq) / (total * width)
     scale = 2.0 / total
@@ -404,10 +370,20 @@
     fresh = jnp.sum(resid * precond, axis=1, keepdims=True)
     direction = precond + fresh / rho * direction
     state = (direction, solution, resid, fresh)
-    direction, solution, rho, local = middle_steps(
-        calib, diag, damping.reshape(1, 1), state, scale, ITERS - 2, nd, nl
+    direction, solution, rho, norms, weights, mask = middle_steps(
+        calib,
+        diag,
+        damping.reshape(1, 1),
+        state,
+        block_weight.T,
+        prune_mask.T.astype(jnp.bfloat16),
+        scale,
+        ITERS - 2,
+        nd,
+        nl,
     )
-    energy = scale * small_sum(local, nd, nl)[0] + damping * jnp.sum(direction * direction, axis=1)
+    weights = weights.reshape(block, -1)
+    energy = scale * norms[0] + damping * jnp.sum(direction * direction, axis=1)
     solution = solution + rho / energy[:, None] * direction
     top = 0.5 * (solution[:, :block] + solution[:, :block].T)
     lower = jnp.linalg.cholesky(top)

time: 305 us -> 301 us (0.987)
    pallas_call x2 -> x1, Pallas kernels: 75.4 us -> 42.2 us  [first_sum(): pl.pallas_call(functools.partial(first_kernel, nd, nl), out_shape=jax.Sha...]
    pallas_call x1, Pallas kernels: 190 us -> 220 us  [middle_steps(): pl.pallas_call(functools.partial(steps_kernel, nd, nl, scale, steps), out...]
where the time goes in v2:
time: 301 us
  Pallas kernels  268 us (89%)
  other arithmetic  22 us (7%)
  matrix products  5.92 us (2%)
  local copies, waits for them, and re-layouts  3.78 us (1%)
    pallas_call x1, Pallas kernels, middle_steps(): pl.pallas_call(functools.partial(steps_kernel, nd, nl, scale, steps), out...  220 us
    pallas_call x1, Pallas kernels, first_sum(): pl.pallas_call(functools.partial(first_kernel, nd, nl), out_shape=jax.Sha...  42.2 us
    another operation x3, other arithmetic, per_device(): lower = jnp.linalg.cholesky(top)  12.4 us

profile of v2, /device:TPU:0, one launch (start us, length us, event | category | flops | bytes accessed | tf_op | source)
XLA Modules:
  0.0 301.1 jit_solution(3263922761404029879)
XLA Ops:
  0.6 0.0 copy-start.1
  0.6 2.6 fusion.1
  3.2 0.1 copy-done.1
  3.3 0.6 multiply_reduce_fusion
  3.9 0.1 select_maximum_fusion.x_ref
  4.0 42.2 %first_sum.1 = f32[128,2816]{1,0:T(8,128)S(1)} custom-call(f32[128,2816]{1,0:T(8,128)S(1)} %select_maximum_fusion.x_ref), custom_call_target="tpu_custom_call" | custom-call | tf_op jit(solution)/shard_map/first_sum/pallas_call | solution.py:155
  46.2 0.6 slice_reduce_fusion
  47.4 0.4 multiply_reduce_fusion.3
  47.9 1.6 multiply_reduce_fusion.2
  49.5 0.0 copy-start.2
  49.5 0.0 copy-start.6
  49.5 0.0 copy-start
  49.6 1.4 multiply_add_fusion.1.d0_ref
  50.9 0.1 copy-done.2
  51.1 0.1 copy.14.rho0_ref
  51.2 0.0 copy-done.6
  51.2 0.1 copy.13
  51.3 0.0 copy-done
  51.3 220.4 %middle_steps.1 = (f32[128,2688]{1,0:T(8,128)}, f32[128,2688]{1,0:T(8,128)}, f32[128,1]{1,0:T(8,128)S(1)}, f32[8,128]{1,0:T(8,128)S(1)}, bf16[8,16,2048]{2,1,0:T...) custom-call(bf16[512,2688]{1,0:T(8,128)(2,1)} %c_ref.1, f32[1,2688]{1,0:T(1,128)S(1)} %bitcast.37, f32[1,1]{1,0:T(1,128)} %bitcast.1.damp_ref, ...), custom_call_target="tpu_custom_call" | custom-call | tf_op jit(solution)/shard_map/middle_steps/pallas_call | solution.py:267
  271.7 0.0 copy-start.3
  271.8 1.6 multiply_reduce_fusion.1
  273.4 0.1 copy.16
  273.5 0.1 copy.15
  273.6 0.1 fusion.5
  273.7 0.0 copy-done.3
  273.7 1.5 multiply_add_fusion
  275.3 0.0 copy-start.4
  275.3 1.1 copy-done.4
  276.4 0.0 copy-start.5
  276.4 0.1 copy.17
  276.5 0.9 fusion.4
  277.4 0.1 copy.18
  277.5 11.7 %cholesky.18 = f32[128,128]{1,0:T(8,128)S(1)} custom-call(f32[128,128]{1,0:T(8,128)S(1)} %fusion.3), custom_call_target="Cholesky" | custom-call | tf_op jit(solution)/shard_map/jit(cholesky)/cholesky | solution.py:389
  289.3 0.6 compare_reduce_fusion
  289.9 0.7 select_select_fusion.l_ref
  290.6 1.1 constant_dynamic-slice_fusion.t_ref
  291.7 5.3 %prune_rows.1 = (bf16[128,2048]{1,0:T(8,128)(2,1)S(1)}, f32[128,2048]{1,0:T(8,128)S(1)}, f32[128,320]{1,0:T(8,128)S(1)}) custom-call(bf16[128,2048]{1,0:T(8,128)(2,1)S(1)} %bitcast.34, bf16[128,2048]{1,0:T(8,128)(2,1)S(1)} %get-tuple-element.12.m_ref, f32[128,128]{1,0:T(8,128)S(1)} %select_select_fusion.l_ref, f32[128,320]{1,0:T(8,128)S(1)} %constant_dynamic-slice_fusion.t_ref), custom_call_target="tpu_custom_call" | custom-call | tf_op jit(solution)/shard_map/prune_rows/pallas_call | solution.py:328
  297.0 0.0 copy-done.5
  297.0 3.4 %fusion = bf16[2048,320]{0,1:T(8,128)(2,1)} fusion(f32[128,2048]{1,0:T(8,128)S(1)} %get-tuple-element.18, f32[128,320]{1,0:T(8,128)S(1)} %get-tuple-element.19, bf16[2048,320]{0,1:T(8,128)(2,1)S(1)} %copy-done.5), kind=kOutput, calls=%fused_computation.2 | convolution fusion | flops 1008599040 | bytes 3833856 | tf_op jit(solution)/shard_map/dot_general | solution.py:396
  300.3 0.7 copy.19
  (12 shorter events, 0.1 us)
Async XLA Ops:
  0.6 2.7 copy-start.1
  49.5 1.5 copy-start.2
  49.5 1.6 copy-start.6
  49.5 1.8 copy-start
  271.7 2.0 copy-start.3
  275.3 1.1 copy-start.4
  276.4 20.6 %copy-start.5 = (bf16[2048,320]{0,1:T(8,128)(2,1)S(1)}, bf16[2048,320]{0,1:T(8,128)(2,1)}, u32[]{:S(2)}) copy-start(bf16[2048,320]{0,1:T(8,128)(2,1)} %param.6) | copy-start | bytes 3932164

commit v3 on v2

--- a/solution.py
+++ b/solution.py
@@ -211,7 +211,7 @@
         return inner[:block] + inner[block:]
 
     def update(g, carry):
-        rows = pl.ds(pl.multiple_of(g * 8, 8), 8)
+        rows = pl.ds(pl.multiple_of(g * 32, 32), 32)
         direction = d_ref[rows, :]
         rho = rho_ref[rows, :]
         image = scale * o_ref[rows, :width] + damp_ref[...] * direction
@@ -240,7 +240,7 @@
             outer = jnp.dot(inner, c_ref[:, cols], preferred_element_type=jnp.float32)
             x_ref[:, cols] = outer[:block] + outer[block:]
         run()
-        lax.fori_loop(0, block // 8, update, 0)
+        lax.fori_loop(0, block // 32, update, 0)
         return carry
 
     lax.fori_loop(0, steps, step, 0)

time: 301 us -> 282 us (0.937)
  Pallas kernels: 268 us -> 249 us
    pallas_call x1, Pallas kernels: 220 us -> 201 us  [middle_steps(): pl.pallas_call(functools.partial(steps_kernel, nd, nl, scale, steps), out...]
where the time goes in v3:
time: 282 us
  Pallas kernels  249 us (88%)
  other arithmetic  22 us (8%)
  matrix products  5.93 us (2%)
  local copies, waits for them, and re-layouts  3.78 us (1%)
    pallas_call x1, Pallas kernels, middle_steps(): pl.pallas_call(functools.partial(steps_kernel, nd, nl, scale, steps), out...  201 us
    pallas_call x1, Pallas kernels, first_sum(): pl.pallas_call(functools.partial(first_kernel, nd, nl), out_shape=jax.Sha...  42.2 us
    another operation x3, other arithmetic, per_device(): lower = jnp.linalg.cholesky(top)  12.4 us

profile of v3, /device:TPU:0, one launch (start us, length us, event | category | flops | bytes accessed | tf_op | source)
XLA Modules:
  0.0 281.9 jit_solution(13117478004123096549)
XLA Ops:
  0.6 0.0 copy-start.1
  0.6 2.6 fusion.1
  3.2 0.1 copy-done.1
  3.3 0.6 multiply_reduce_fusion
  3.9 0.1 select_maximum_fusion.x_ref
  4.0 42.2 %first_sum.1 = f32[128,2816]{1,0:T(8,128)S(1)} custom-call(f32[128,2816]{1,0:T(8,128)S(1)} %select_maximum_fusion.x_ref), custom_call_target="tpu_custom_call" | custom-call | tf_op jit(solution)/shard_map/first_sum/pallas_call | solution.py:155
  46.2 0.6 slice_reduce_fusion
  47.4 0.4 multiply_reduce_fusion.3
  47.9 1.6 multiply_reduce_fusion.2
  49.5 0.0 copy-start.2
  49.5 0.0 copy-start.6
  49.5 0.0 copy-start
  49.6 1.4 multiply_add_fusion.1.d0_ref
  50.9 0.1 copy-done.2
  51.1 0.1 copy.14.rho0_ref
  51.2 0.0 copy-done.6
  51.2 0.1 copy.13
  51.3 0.0 copy-done
  51.3 201.3 %middle_steps.1 = (f32[128,2688]{1,0:T(8,128)}, f32[128,2688]{1,0:T(8,128)}, f32[128,1]{1,0:T(8,128)S(1)}, f32[8,128]{1,0:T(8,128)S(1)}, bf16[8,16,2048]{2,1,0:T...) custom-call(bf16[512,2688]{1,0:T(8,128)(2,1)} %c_ref.1, f32[1,2688]{1,0:T(1,128)S(1)} %bitcast.37, f32[1,1]{1,0:T(1,128)} %bitcast.1.damp_ref, ...), custom_call_target="tpu_custom_call" | custom-call | tf_op jit(solution)/shard_map/middle_steps/pallas_call | solution.py:267
  252.6 0.0 copy-start.3
  252.6 1.6 multiply_reduce_fusion.1
  254.2 0.1 copy.16
  254.4 0.1 copy.15
  254.5 0.1 fusion.5
  254.6 0.0 copy-done.3
  254.6 1.5 multiply_add_fusion
  256.1 0.0 copy-start.4
  256.2 1.1 copy-done.4
  257.2 0.0 copy-start.5
  257.2 0.1 copy.17
  257.3 0.9 fusion.4
  258.3 0.1 copy.18
  258.4 11.7 %cholesky.18 = f32[128,128]{1,0:T(8,128)S(1)} custom-call(f32[128,128]{1,0:T(8,128)S(1)} %fusion.3), custom_call_target="Cholesky" | custom-call | tf_op jit(solution)/shard_map/jit(cholesky)/cholesky | solution.py:389
  270.1 0.6 compare_reduce_fusion
  270.8 0.7 select_select_fusion.l_ref
  271.4 1.1 constant_dynamic-slice_fusion.t_ref
  272.5 5.3 %prune_rows.1 = (bf16[128,2048]{1,0:T(8,128)(2,1)S(1)}, f32[128,2048]{1,0:T(8,128)S(1)}, f32[128,320]{1,0:T(8,128)S(1)}) custom-call(bf16[128,2048]{1,0:T(8,128)(2,1)S(1)} %bitcast.34, bf16[128,2048]{1,0:T(8,128)(2,1)S(1)} %get-tuple-element.12.m_ref, f32[128,128]{1,0:T(8,128)S(1)} %select_select_fusion.l_ref, f32[128,320]{1,0:T(8,128)S(1)} %constant_dynamic-slice_fusion.t_ref), custom_call_target="tpu_custom_call" | custom-call | tf_op jit(solution)/shard_map/prune_rows/pallas_call | solution.py:328
  277.8 0.0 copy-done.5
  277.8 3.4 %fusion = bf16[2048,320]{0,1:T(8,128)(2,1)} fusion(f32[128,2048]{1,0:T(8,128)S(1)} %get-tuple-element.18, f32[128,320]{1,0:T(8,128)S(1)} %get-tuple-element.19, bf16[2048,320]{0,1:T(8,128)(2,1)S(1)} %copy-done.5), kind=kOutput, calls=%fused_computation.2 | convolution fusion | flops 1008599040 | bytes 3833856 | tf_op jit(solution)/shard_map/dot_general | solution.py:396
  281.2 0.7 copy.19
  (12 shorter events, 0.1 us)
Async XLA Ops:
  0.6 2.7 copy-start.1
  49.5 1.5 copy-start.2
  49.5 1.6 copy-start.6
  49.5 1.8 copy-start
  252.6 2.0 copy-start.3
  256.1 1.1 copy-start.4
  257.2 20.6 %copy-start.5 = (bf16[2048,320]{0,1:T(8,128)(2,1)S(1)}, bf16[2048,320]{0,1:T(8,128)(2,1)}, u32[]{:S(2)}) copy-start(bf16[2048,320]{0,1:T(8,128)(2,1)} %param.6) | copy-start | bytes 3932164

commit v4 on v3

--- a/solution.py
+++ b/solution.py
@@ -211,7 +211,7 @@
         return inner[:block] + inner[block:]
 
     def update(g, carry):
-        rows = pl.ds(pl.multiple_of(g * 32, 32), 32)
+        rows = pl.ds(pl.multiple_of(g * 64, 64), 64)
         direction = d_ref[rows, :]
         rho = rho_ref[rows, :]
         image = scale * o_ref[rows, :width] + damp_ref[...] * direction
@@ -240,7 +240,7 @@
             outer = jnp.dot(inner, c_ref[:, cols], preferred_element_type=jnp.float32)
             x_ref[:, cols] = outer[:block] + outer[block:]
         run()
-        lax.fori_loop(0, block // 32, update, 0)
+        lax.fori_loop(0, block // 64, update, 0)
         return carry
 
     lax.fori_loop(0, steps, step, 0)

time: 282 us -> 279 us (0.989)
  Pallas kernels: 249 us -> 245 us
    pallas_call x1, Pallas kernels: 201 us -> 198 us  [middle_steps(): pl.pallas_call(functools.partial(steps_kernel, nd, nl, scale, steps), out...]
where the time goes in v4:
time: 279 us
  Pallas kernels  245 us (88%)
  other arithmetic  22 us (8%)
  matrix products  5.92 us (2%)
  local copies, waits for them, and re-layouts  3.78 us (1%)
    pallas_call x1, Pallas kernels, middle_steps(): pl.pallas_call(functools.partial(steps_kernel, nd, nl, scale, steps), out...  198 us
    pallas_call x1, Pallas kernels, first_sum(): pl.pallas_call(functools.partial(first_kernel, nd, nl), out_shape=jax.Sha...  42.2 us
    another operation x3, other arithmetic, per_device(): lower = jnp.linalg.cholesky(top)  12.4 us

profile of v4, /device:TPU:0, one launch (start us, length us, event | category | flops | bytes accessed | tf_op | source)
XLA Modules:
  0.0 278.7 jit_solution(15236667587447604143)
XLA Ops:
  0.6 0.0 copy-start.1
  0.6 2.6 fusion.1
  3.2 0.1 copy-done.1
  3.3 0.6 multiply_reduce_fusion
  3.9 0.1 select_maximum_fusion.x_ref
  4.0 42.2 %first_sum.1 = f32[128,2816]{1,0:T(8,128)S(1)} custom-call(f32[128,2816]{1,0:T(8,128)S(1)} %select_maximum_fusion.x_ref), custom_call_target="tpu_custom_call" | custom-call | tf_op jit(solution)/shard_map/first_sum/pallas_call | solution.py:155
  46.2 0.6 slice_reduce_fusion
  47.4 0.4 multiply_reduce_fusion.3
  47.9 1.6 multiply_reduce_fusion.2
  49.5 0.0 copy-start.2
  49.5 0.0 copy-start.6
  49.5 0.0 copy-start
  49.6 1.4 multiply_add_fusion.1.d0_ref
  50.9 0.1 copy-done.2
  51.1 0.1 copy.14.rho0_ref
  51.2 0.0 copy-done.6
  51.2 0.1 copy.13
  51.3 0.0 copy-done
  51.3 198.1 %middle_steps.1 = (f32[128,2688]{1,0:T(8,128)}, f32[128,2688]{1,0:T(8,128)}, f32[128,1]{1,0:T(8,128)S(1)}, f32[8,128]{1,0:T(8,128)S(1)}, bf16[8,16,2048]{2,1,0:T...) custom-call(bf16[512,2688]{1,0:T(8,128)(2,1)} %c_ref.1, f32[1,2688]{1,0:T(1,128)S(1)} %bitcast.37, f32[1,1]{1,0:T(1,128)} %bitcast.1.damp_ref, ...), custom_call_target="tpu_custom_call" | custom-call | tf_op jit(solution)/shard_map/middle_steps/pallas_call | solution.py:267
  249.4 0.0 copy-start.3
  249.4 1.6 multiply_reduce_fusion.1
  251.0 0.1 copy.16
  251.1 0.1 copy.15
  251.2 0.1 fusion.5
  251.4 0.0 copy-done.3
  251.4 1.5 multiply_add_fusion
  252.9 0.0 copy-start.4
  252.9 1.1 copy-done.4
  254.0 0.0 copy-start.5
  254.0 0.1 copy.17
  254.1 0.9 fusion.4
  255.0 0.1 copy.18
  255.2 11.7 %cholesky.18 = f32[128,128]{1,0:T(8,128)S(1)} custom-call(f32[128,128]{1,0:T(8,128)S(1)} %fusion.3), custom_call_target="Cholesky" | custom-call | tf_op jit(solution)/shard_map/jit(cholesky)/cholesky | solution.py:389
  266.9 0.6 compare_reduce_fusion
  267.5 0.7 select_select_fusion.l_ref
  268.2 1.1 constant_dynamic-slice_fusion.t_ref
  269.3 5.3 %prune_rows.1 = (bf16[128,2048]{1,0:T(8,128)(2,1)S(1)}, f32[128,2048]{1,0:T(8,128)S(1)}, f32[128,320]{1,0:T(8,128)S(1)}) custom-call(bf16[128,2048]{1,0:T(8,128)(2,1)S(1)} %bitcast.34, bf16[128,2048]{1,0:T(8,128)(2,1)S(1)} %get-tuple-element.12.m_ref, f32[128,128]{1,0:T(8,128)S(1)} %select_select_fusion.l_ref, f32[128,320]{1,0:T(8,128)S(1)} %constant_dynamic-slice_fusion.t_ref), custom_call_target="tpu_custom_call" | custom-call | tf_op jit(solution)/shard_map/prune_rows/pallas_call | solution.py:328
  274.6 0.0 copy-done.5
  274.6 3.4 %fusion = bf16[2048,320]{0,1:T(8,128)(2,1)} fusion(f32[128,2048]{1,0:T(8,128)S(1)} %get-tuple-element.18, f32[128,320]{1,0:T(8,128)S(1)} %get-tuple-element.19, bf16[2048,320]{0,1:T(8,128)(2,1)S(1)} %copy-done.5), kind=kOutput, calls=%fused_computation.2 | convolution fusion | flops 1008599040 | bytes 3833856 | tf_op jit(solution)/shard_map/dot_general | solution.py:396
  278.0 0.7 copy.19
  (12 shorter events, 0.1 us)
Async XLA Ops:
  0.6 2.7 copy-start.1
  49.5 1.5 copy-start.2
  49.5 1.6 copy-start.6
  49.5 1.8 copy-start
  249.4 2.0 copy-start.3
  252.9 1.1 copy-start.4
  254.0 20.6 %copy-start.5 = (bf16[2048,320]{0,1:T(8,128)(2,1)S(1)}, bf16[2048,320]{0,1:T(8,128)(2,1)}, u32[]{:S(2)}) copy-start(bf16[2048,320]{0,1:T(8,128)(2,1)} %param.6) | copy-start | bytes 3932164
